TPU v7x, 128 devices: a whole 4x4x4 slice. The times are simulated.
128 devices in a mesh: lev: 8 (over x, z_lo), mem: 16 (over z_hi, y, core).
Axes of the slice: x: 4, y: 4, z: 4 (z_hi: 2, z_lo: 2; z = z_hi * 2 + z_lo), core: 2. Of those that a mesh axis runs over, the one named last changes fastest.
Arguments:
- control: float32 [4096, 128, 128], P(None, 'mem', 'lev'), may hold values from -6 to 6
- perturb: bfloat16 [4096, 128, 5, 128], P('lev', 'mem'), may hold values from -6 to 6
- member_weights: float32 [128], P('mem'), may hold values from 0.25 to 4
- blocks: bfloat16 [64, 16, 64, 64], P(None, 'mem'), may hold values from -0.1875 to 0.1875
- block_cols: int32 [64, 16], replicated, may hold values from 0 to 63, as said below
- vertical: float32 [128, 128], replicated, may hold values from -4 to 4
Outputs:
- increment: float32 [4096, 5, 128], P(('lev', 'mem'))
Inputs may be any that keep to these rules, and one draw needn't show every extreme that they name: Within a block row the 16 block columns are distinct, and for every j the column block_cols[:, j] names each of the 64 block rows exactly once.
All inputs are finite; a program needn't handle non-finite values.
Results may differ from a plain program's by a relative error of at most 0.0003.
Values may be sent and summed in bfloat16 or wider, within the bound.
No kernel may reach another device: no remote copies, remote signals or barrier semaphores. Data moves between devices by JAX's collectives and lax.ppermute only.
A program may use at most 192 MiB of HBM per device.

v0:
```python
import functools
import math

import jax
import jax.numpy as jnp
from jax import lax
from jax.experimental import pallas as pl
from jax.experimental.pallas import tpu as pltpu
from jax.sharding import Mesh
from jax.sharding import PartitionSpec as P

BF = jnp.bfloat16
F32 = jnp.float32
AXES = ("x", "zlo", "zhi", "y", "core")


def coords(d):
    x, zlo, zhi, y, c = d // 32, d // 16 % 2, d // 8 % 2, d // 2 % 4, d % 2
    return x, y, 2 * zhi + zlo, c


def device(x, y, z, c):
    return (x % 4) * 32 + (z % 2) * 16 + (z // 2) * 8 + (y % 4) * 2 + c


def perm(move):
    return [(d, device(*move(*coords(d)))) for d in range(128)]


Z_NEAR = perm(lambda x, y, z, c: (x, y, 3 - z, c))
Y_UP = perm(lambda x, y, z, c: (x, y + 1, z, c))
Y_DOWN = perm(lambda x, y, z, c: (x, y - 1, z, c))
Y_FAR = perm(lambda x, y, z, c: (x, y + 2, z, c))
CORE = perm(lambda x, y, z, c: (x, y, z, 1 - c))
LIMIT = 20 * 1024 * 1024
VMEM = pl.BlockSpec(memory_space=pltpu.VMEM)
SMEM = pl.BlockSpec(memory_space=pltpu.SMEM)


def send(value, pairs):
    return lax.ppermute(value, AXES, pairs)


def split2(x):
    hi = x.astype(BF)
    return hi, (x - hi.astype(F32)).astype(BF)


def pack_kernel(half_ref, b_ref, o_ref):
    rows = o_ref.shape[0]
    for t in range(rows):
        i = 2 * (half_ref[0] * rows + t)
        two = jnp.concatenate([b_ref[i], b_ref[i + 1]], axis=0).astype(F32)
        o_ref[t] = two.T.astype(BF)


def pack(half, b):
    n, p, q = b.shape
    return pl.pallas_call(
        pack_kernel,
        out_shape=jax.ShapeDtypeStruct((n // 4, q, 2 * p), BF),
        in_specs=[SMEM, VMEM],
        out_specs=VMEM,
        compiler_params=pltpu.CompilerParams(vmem_limit_bytes=LIMIT),
    )(half, b)


def prep_kernel(core_ref, own_ref, other_ref, o_ref):
    core = core_ref[0]
    columns, width = own_ref.shape
    for ref, c in ((own_ref, core), (other_ref, 1 - core)):
        value = ref[...]
        for owner in range(2):
            begin = [64 * b + 32 * owner for b in range(width // 64)]
            runs = jnp.concatenate([value[:, b : b + 32] for b in begin], axis=1)
            hi, lo = split2(runs)
            o_ref[owner, pl.ds(pl.multiple_of(c * columns, columns), columns)] = hi
            o_ref[owner, pl.ds(pl.multiple_of((2 + c) * columns, columns), columns)] = lo


def prep_call(core, own, other):
    columns, n_all = own.shape
    width = 1024
    return pl.pallas_call(
        prep_kernel,
        grid=(n_all // width,),
        out_shape=jax.ShapeDtypeStruct((2, 4 * columns, n_all // 2), BF),
        in_specs=[SMEM] + [pl.BlockSpec((columns, width), lambda g: (0, g))] * 2,
        out_specs=pl.BlockSpec((2, 4 * columns, width // 2), lambda g: (0, 0, g)),
        compiler_params=pltpu.CompilerParams(vmem_limit_bytes=LIMIT),
    )(core, own, other)


def place_kernel(slots, cols_ref, core_ref, jtab_ref, *rest):
    pieces, bt = rest[: len(slots)], rest[-1]
    n_half, lanes = bt.shape[1:]
    first = core_ref[0] * (cols_ref.shape[0] // 2)
    if len(rest) == len(slots) + 1:

        def zero(r, _):
            s = pl.ds(pl.multiple_of(r * 64, 64), 64)
            bt[0, s] = jnp.zeros((64, lanes), BF)
            bt[1, s] = jnp.zeros((64, lanes), BF)
            return 0

        lax.fori_loop(0, n_half // 64, zero, 0)
    for piece, slot in zip(pieces, slots):
        for s in range(piece.shape[0]):
            j = jtab_ref[slot + s]
            for t in range(piece.shape[1]):
                tile = piece[s, t]
                for h in range(2):
                    row = pl.multiple_of(cols_ref[first + 2 * t + h, j] * 32, 32)
                    lane = t * 128 + h * 64
                    for owner in range(2):
                        part = tile[owner * 32 : owner * 32 + 32, h * 64 : h * 64 + 64]
                        bt[owner, pl.ds(row, 32), lane : lane + 64] = part


def place_call(cols, core, jtab, pieces, slots, shape, dense=None):
    given = () if dense is None else (dense,)
    position = 3 + len(pieces)
    return pl.pallas_call(
        functools.partial(place_kernel, slots),
        out_shape=jax.ShapeDtypeStruct(shape, BF),
        in_specs=[SMEM] * 3 + [VMEM] * (len(pieces) + len(given)),
        out_specs=VMEM,
        input_output_aliases={position: 0} if given else {},
        compiler_params=pltpu.CompilerParams(vmem_limit_bytes=LIMIT),
    )(cols, core, jtab, *pieces, *given)


def forward_kernel(x_ref, bt, f_ref):
    columns = x_ref.shape[1] // 2
    width = 1024

    def step(n, _):
        s = pl.ds(pl.multiple_of(n * width, width), width)
        f = jnp.dot(x_ref[0], bt[0, :, s], preferred_element_type=F32)
        f += jnp.dot(x_ref[1], bt[1, :, s], preferred_element_type=F32)
        hi, lo = split2(f[:columns] + f[columns:])
        f_ref[0:columns, s] = hi
        f_ref[columns:, s] = lo
        return 0

    lax.fori_loop(0, bt.shape[2] // width, step, 0)


def backward_kernel(owner_ref, f_ref, bt, o_ref):
    groups, columns, width = o_ref.shape
    per = 4

    def step(n, _):
        s = pl.ds(pl.multiple_of(n * per * width, per * width), per * width)
        y = lax.dot_general(
            f_ref[...], bt[owner_ref[0], s], (((1,), (1,)), ((), ())), preferred_element_type=F32
        )
        y = y[:columns] + y[columns:]
        for g in range(per):
            o_ref[per * n + g] = y[:, g * width : (g + 1) * width]
        return 0

    lax.fori_loop(0, groups // per, step, 0)


def forward_call(x, dense):
    lanes = dense.shape[2]
    flops = 4 * x.shape[1] * x.shape[2] * lanes
    return pl.pallas_call(
        forward_kernel,
        out_shape=jax.ShapeDtypeStruct((x.shape[1], lanes), BF),
        in_specs=[VMEM, VMEM],
        out_specs=VMEM,
        compiler_params=pltpu.CompilerParams(vmem_limit_bytes=LIMIT),
        cost_estimate=pl.CostEstimate(flops=flops, bytes_accessed=8 << 20, transcendentals=0),
    )(x, dense)


def backward_call(owner, f, dense, groups):
    n_half, lanes = dense.shape[1:]
    flops = 2 * f.shape[0] * n_half * lanes
    return pl.pallas_call(
        backward_kernel,
        out_shape=jax.ShapeDtypeStruct((groups, f.shape[0] // 2, n_half // groups), F32),
        in_specs=[SMEM, VMEM, VMEM],
        out_specs=VMEM,
        compiler_params=pltpu.CompilerParams(vmem_limit_bytes=LIMIT),
        cost_estimate=pl.CostEstimate(flops=flops, bytes_accessed=4 << 20, transcendentals=0),
    )(owner, f, dense)


def post_kernel(core_ref, w_own_ref, w_other_ref, y_ref, v_ref, own_ref, other_ref, o_ref, loc):
    core = core_ref[0]
    groups = y_ref.shape[0]
    block = loc.shape[1]
    nodes = pl.ds(pl.multiple_of(pl.program_id(0) * block, block), block)
    members = w_own_ref.shape[0]
    inner = v_ref.shape[1] // groups
    vhi, vlo = split2(v_ref[...])
    dims = (((1,), (1,)), ((), ()))
    for m in range(2 * members):
        rows = slice(m * inner, (m + 1) * inner)
        column = jnp.concatenate([y_ref[s, rows, nodes] for s in range(groups)], axis=0)
        hi, lo = split2(column.T)
        part = lax.dot_general(hi, vhi, dims, preferred_element_type=F32)
        part += lax.dot_general(lo, vhi, dims, preferred_element_type=F32)
        part += lax.dot_general(hi, vlo, dims, preferred_element_type=F32)
        c, k = divmod(m, members)
        loc[c, :, k, :] = part * jnp.where(core == c, w_own_ref[k], w_other_ref[k])
    _, nvar, owned, _ = o_ref.shape
    for d in range(o_ref.shape[0]):
        rows = pl.ds(d * owned, owned)
        near = loc[core, rows]
        far = loc[1 - core, rows]
        for v in range(nvar):
            both = own_ref[d, 0, :, v].astype(F32) * near
            both += other_ref[d, 0, :, v].astype(F32) * far
            o_ref[d, v] = jnp.sum(both, axis=1)


def post_call(core, w_own, w_other, y, v, own, other):
    parts, _, owned, nvar, members, levels = own.shape
    _, _, nodes = y.shape
    block = 128
    step = block // owned
    grid_spec = pltpu.PrefetchScalarGridSpec(
        num_scalar_prefetch=1,
        grid=(nodes // block,),
        in_specs=[
            SMEM,
            SMEM,
            VMEM,
            pl.BlockSpec((levels, levels), lambda g, c: (0, 0)),
            pl.BlockSpec(
                (step, 1, owned, nvar, members, levels), lambda g, c: (g, c[0], 0, 0, 0, 0)
            ),
            pl.BlockSpec(
                (step, 1, owned, nvar, members, levels), lambda g, c: (g, c[0], 0, 0, 0, 0)
            ),
        ],
        out_specs=pl.BlockSpec((step, nvar, owned, levels), lambda g, c: (g, 0, 0, 0)),
        scratch_shapes=[pltpu.VMEM((2, block, members, levels), F32)],
    )
    return pl.pallas_call(
        post_kernel,
        grid_spec=grid_spec,
        out_shape=jax.ShapeDtypeStruct((parts, nvar, owned, levels), F32),
        compiler_params=pltpu.CompilerParams(vmem_limit_bytes=LIMIT),
    )(core, w_own, w_other, y, v, own, other)


LAYOUT = ((0, 0), (0, 1), (3, 0), (1, 0), (2, 0), (3, 1), (1, 1), (2, 1))


STAGES = ((0,), (1, 2, 3), (4,), (5, 6, 7))


def gather(unit):
    near = send(unit, Z_NEAR)
    up = send(unit, Y_UP)
    down = send(unit, Y_DOWN)
    far = send(unit, Y_FAR)
    near_up = send(near, Y_UP)
    near_down = send(near, Y_DOWN)
    near_far = send(far, Z_NEAR)
    return [unit, near, up, down, far, near_up, near_down, near_far]


def slot_table():
    zhi, y, c = lax.axis_index("zhi"), lax.axis_index("y"), lax.axis_index("core")
    slot = jnp.arange(16, dtype=jnp.int32)
    dy, dz = (sum(jnp.where(slot // 2 == i, d[n], 0) for i, d in enumerate(LAYOUT)) for n in (0, 1))
    return ((zhi ^ dz) * 8 + ((y + dy) & 3) * 2 + (c ^ (slot & 1))).astype(jnp.int32)


def shards(control, perturb, member_weights, blocks, block_cols, vertical):
    nodes_all, mem_dev, lev_dev = control.shape
    members_all = mem_dev * 16
    groups, owned = 8, nodes_all // 128
    core_index = lax.axis_index("core")
    core = core_index.reshape(1).astype(jnp.int32)
    other = 1 - core
    stored = blocks[:, 0]
    handed = send(pack(other, stored), CORE)
    pieces = gather(jnp.stack([pack(core, stored), handed]))
    x = control.transpose(1, 2, 0).reshape(mem_dev * lev_dev, nodes_all)
    x_other = send(x, CORE)
    xc = prep_call(core, x, x_other)
    weights = member_weights / math.sqrt(members_all - 1)
    weights_other = send(weights, CORE)
    fields = perturb.transpose(0, 2, 1, 3)
    fields_other = send(fields, CORE)
    shape = (groups, 2, owned) + fields.shape[1:]
    fields, fields_other = fields.reshape(shape), fields_other.reshape(shape)
    table = slot_table()
    shape = (2, nodes_all // 2, nodes_all // 2)
    dense = None
    for part in STAGES:
        slots = tuple(2 * p for p in part)
        some = [pieces[p] for p in part]
        dense = place_call(block_cols, core, table, some, slots, shape, dense)
    f = forward_call(xc, dense)
    give = backward_call(other, f, dense, groups)
    keep = backward_call(core, f, dense, groups)
    y = keep + send(give, CORE)
    y = lax.all_to_all(y, ("x", "zlo"), split_axis=0, concat_axis=0, tiled=True)
    out = post_call(core, weights, weights_other, y, vertical, fields, fields_other)
    out = lax.all_to_all(out, ("zhi", "y"), split_axis=0, concat_axis=0, tiled=True)
    return jnp.sum(out, axis=0).transpose(1, 0, 2)


def solution(mesh):
    fine = Mesh(mesh.devices.reshape(4, 2, 2, 4, 2), AXES)
    lev, mem = ("x", "zlo"), ("zhi", "y", "core")
    in_specs = (
        P(None, mem, lev),
        P(lev, mem, None, None),
        P(mem),
        P(None, mem, None, None),
        P(),
        P(),
    )
    out_specs = P(AXES, None, None)

    return jax.shard_map(shards, mesh=fine, in_specs=in_specs, out_specs=out_specs, check_vma=False)
```

profile of v0, /device:TPU:0, one launch (start us, length us, event | category | flops | bytes accessed | tf_op | source)
XLA Modules:
  0.0 138.2 jit_solution(12031254341154032667)
XLA Ops:
  0.0 0.0 copy-start.6
  0.0 0.0 collective-permute-start.1
  0.0 0.0 copy-start.1
  0.0 1.2 copy-done.1
  1.2 0.2 shard_map.66
  1.4 0.6 collective-permute-start.2
  2.0 0.2 shard_map.65
  2.2 2.5 %collective-permute-done.2 = bf16[16,64,128]{2,1,0:T(8,128)(2,1)S(1)} collective-permute-done((bf16[16,64,128]{2,1,0:T(8,128)(2,1)S(1)}, bf16[16,64,128]{2,1,0:T(8,128)(2,1)S(1)}, u32[]{:S(2)}, u32[]{:S(2)}) %collective-permute-start.2) | collective-permute-done | bytes 262176 | tf_op jit(solution)/shard_map/ppermute | solution.py:41
  4.7 0.1 pad_maximum_fusion.rest_0_
  4.8 4.2 %collective-permute-start.3 = (bf16[2,16,64,128]{3,2,1,0:T(8,128)(2,1)S(1)}, bf16[2,16,64,128]{3,2,1,0:T(8,128)(2,1)S(1)}, u32[]{:S(2)}, u32[]{:S(2)}) collective-permute-start(bf16[2,16,64,128]{3,2,1,0:T(8,128)(2,1)S(1)} %pad_maximum_fusion.rest_0_), channel_id=1, source_target_pairs={{0,24},{1,25},{2,26},{3,27},{4,28},{5,29},{6,30},{7,31},{8,16},{9,... | collective-permute-start | bytes 1572872 | tf_op jit(solution)/shard_map/ppermute | solution.py:41
  9.0 1.6 %collective-permute-start.8 = (bf16[2,16,64,128]{3,2,1,0:T(8,128)(2,1)S(1)}, bf16[2,16,64,128]{3,2,1,0:T(8,128)(2,1)S(1)}, u32[]{:S(2)}, u32[]{:S(2)}) collective-permute-start(bf16[2,16,64,128]{3,2,1,0:T(8,128)(2,1)S(1)} %pad_maximum_fusion.rest_0_), channel_id=1, source_target_pairs={{0,2},{1,3},{2,4},{3,5},{4,6},{5,7},{6,0},{7,1},{8,10},{9,11},{10,... | collective-permute-start | bytes 1572872 | tf_op jit(solution)/shard_map/ppermute | solution.py:41
  10.6 2.9 %collective-permute-start.6 = (bf16[2,16,64,128]{3,2,1,0:T(8,128)(2,1)S(1)}, bf16[2,16,64,128]{3,2,1,0:T(8,128)(2,1)}, u32[]{:S(2)}, u32[]{:S(2)}) collective-permute-start(bf16[2,16,64,128]{3,2,1,0:T(8,128)(2,1)S(1)} %pad_maximum_fusion.rest_0_), channel_id=1, source_target_pairs={{0,4},{1,5},{2,6},{3,7},{4,0},{5,1},{6,2},{7,3},{8,12},{9,13},{10,... | collective-permute-start | bytes 1572872 | tf_op jit(solution)/shard_map/ppermute | solution.py:41
  13.5 1.3 collective-permute-start.9
  14.9 6.4 %collective-permute-done.3.rest_0_ = bf16[2,16,64,128]{3,2,1,0:T(8,128)(2,1)S(1)} collective-permute-done((bf16[2,16,64,128]{3,2,1,0:T(8,128)(2,1)S(1)}, bf16[2,16,64,128]{3,2,1,0:T(8,128)(2,1)S(1)}, u32[]{:S(2)}, u32[]{:S(2)}) %collective-permute-start.3) | collective-permute-done | bytes 524320 | tf_op jit(solution)/shard_map/ppermute | solution.py:41
  21.3 1.6 %collective-permute-start.4 = (bf16[2,16,64,128]{3,2,1,0:T(8,128)(2,1)S(1)}, bf16[2,16,64,128]{3,2,1,0:T(8,128)(2,1)}, u32[]{:S(2)}, u32[]{:S(2)}) collective-permute-start(bf16[2,16,64,128]{3,2,1,0:T(8,128)(2,1)S(1)} %collective-permute-done.3.rest_0_), channel_id=1, source_target_pairs={{0,2},{1,3},{2,4},{3,5},{4,6},{5,7},{6,0},{7,1},{8,10},{9,11},{10,... | collective-permute-start | bytes 1572872 | tf_op jit(solution)/shard_map/ppermute | solution.py:41
  22.8 1.2 collective-permute-done.8.rest_1_
  24.0 0.0 copy-start.3
  24.0 0.8 copy-done.3
  24.8 2.9 %collective-permute-start.5 = (bf16[2,16,64,128]{3,2,1,0:T(8,128)(2,1)S(1)}, bf16[2,16,64,128]{3,2,1,0:T(8,128)(2,1)}, u32[]{:S(2)}, u32[]{:S(2)}) collective-permute-start(bf16[2,16,64,128]{3,2,1,0:T(8,128)(2,1)S(1)} %collective-permute-done.3.rest_0_), channel_id=1, source_target_pairs={{0,6},{1,7},{2,0},{3,1},{4,2},{5,3},{6,4},{7,5},{8,14},{9,15},{10,... | collective-permute-start | bytes 1572872 | tf_op jit(solution)/shard_map/ppermute | solution.py:41
  27.7 10.0 %collective-permute-done.6.rest_0_ = bf16[2,16,64,128]{3,2,1,0:T(8,128)(2,1)} collective-permute-done((bf16[2,16,64,128]{3,2,1,0:T(8,128)(2,1)S(1)}, bf16[2,16,64,128]{3,2,1,0:T(8,128)(2,1)}, u32[]{:S(2)}, u32[]{:S(2)}) %collective-permute-start.6) | collective-permute-done | bytes 524320 | tf_op jit(solution)/shard_map/ppermute | solution.py:41
  37.7 0.1 collective-permute-start.7
  37.7 0.0 copy-done.6
  37.7 0.1 copy.13.cols_ref
  37.8 0.0 collective-permute-done.9.rest_2_
  37.8 0.1 collective-permute-start.11
  37.9 0.0 copy-start.4
  38.0 2.5 %shard_map.67.rest_3_ = bf16[2,2048,2048]{2,1,0:T(8,128)(2,1)S(1)} custom-call(s32[64,16]{1,0:T(8,128)S(1)} %copy.13.cols_ref, s32[1]{0:T(128)} %bitcast.core_ref.half_ref.owner_ref, s32[16]{0:T(128)S(1)} %fusion.1.jtab_ref, bf16[2,16,64,128]{3,2,1,0:T(8,128)(2,1)S(1)} %pad_maximum_fusion.rest_0_), custom_call_target="tpu_custom_call" | custom-call | tf_op jit(solution)/shard_map/pallas_call | solution.py:123
  40.4 0.0 copy-done.4
  40.4 2.1 %shard_map.68.rest_1_ = bf16[2,2048,2048]{2,1,0:T(8,128)(2,1)S(1)} custom-call(s32[64,16]{1,0:T(8,128)S(1)} %copy.13.cols_ref, s32[1]{0:T(128)} %bitcast.core_ref.half_ref.owner_ref, s32[16]{0:T(128)S(1)} %fusion.1.jtab_ref, bf16[2,16,64,128]{3,2,1,0:T(8,128)(2,1)S(1)} %collective-permute-done.3.rest_0_, ...), custom_call_target="tpu_custom_call", output_to_operand_aliasing={{}: (6, {})} | custom-call | tf_op jit(solution)/shard_map/pallas_call | solution.py:123
  42.6 1.3 shard_map.69.rest_3_
  43.9 0.0 copy-start.2
  43.9 3.1 %collective-permute-done.4.rest_0_ = bf16[2,16,64,128]{3,2,1,0:T(8,128)(2,1)} collective-permute-done((bf16[2,16,64,128]{3,2,1,0:T(8,128)(2,1)S(1)}, bf16[2,16,64,128]{3,2,1,0:T(8,128)(2,1)}, u32[]{:S(2)}, u32[]{:S(2)}) %collective-permute-start.4) | collective-permute-done | bytes 524320 | tf_op jit(solution)/shard_map/ppermute | solution.py:41
  47.0 0.2 collective-permute-done.5.rest_1_
  47.2 3.7 %collective-permute-done.7.rest_2_ = bf16[2,16,64,128]{3,2,1,0:T(8,128)(2,1)} collective-permute-done((bf16[2,16,64,128]{3,2,1,0:T(8,128)(2,1)}, bf16[2,16,64,128]{3,2,1,0:T(8,128)(2,1)}, u32[]{:S(2)}, u32[]{:S(2)}) %collective-permute-start.7) | collective-permute-done | bytes 524320 | tf_op jit(solution)/shard_map/ppermute | solution.py:41
  50.9 2.4 %shard_map.70.bt = bf16[2,2048,2048]{2,1,0:T(8,128)(2,1)S(1)} custom-call(s32[64,16]{1,0:T(8,128)S(1)} %copy.13.cols_ref, s32[1]{0:T(128)} %bitcast.core_ref.half_ref.owner_ref, s32[16]{0:T(128)S(1)} %fusion.1.jtab_ref, bf16[2,16,64,128]{3,2,1,0:T(8,128)(2,1)} %collective-permute-done.4.rest_0_, ...), custom_call_target="tpu_custom_call", output_to_operand_aliasing={{}: (6, {})} | custom-call | tf_op jit(solution)/shard_map/pallas_call | solution.py:123
  53.3 0.0 collective-permute-done.1.other_ref
  53.3 0.0 copy-done.2
  53.3 3.3 %shard_map.64.x_ref = bf16[2,512,2048]{2,1,0:T(8,128)(2,1)S(1)} custom-call(s32[1]{0:T(128)} %bitcast.core_ref.half_ref.owner_ref, f32[128,4096]{1,0:T(8,128)S(1)} %bitcast.17, f32[128,4096]{1,0:T(8,128)S(1)} %collective-permute-done.1.other_ref), custom_call_target="tpu_custom_call" | custom-call | tf_op jit(solution)/shard_map/pallas_call | solution.py:84
  56.6 9.0 %shard_map.71.f_ref = bf16[512,2048]{1,0:T(8,128)(2,1)S(1)} custom-call(bf16[2,512,2048]{2,1,0:T(8,128)(2,1)S(1)} %shard_map.64.x_ref, bf16[2,2048,2048]{2,1,0:T(8,128)(2,1)S(1)} %shard_map.70.bt), custom_call_target="tpu_custom_call" | custom-call | flops 8589934592 | bytes 8388608 | tf_op jit(solution)/shard_map/pallas_call | solution.py:169
  65.6 4.7 %shard_map.73 = f32[8,256,256]{2,1,0:T(8,128)S(1)} custom-call(s32[1]{0:T(128)S(6)} %sub.25.half_ref.owner_ref, bf16[512,2048]{1,0:T(8,128)(2,1)S(1)} %shard_map.71.f_ref, bf16[2,2048,2048]{2,1,0:T(8,128)(2,1)S(1)} %shard_map.70.bt), custom_call_target="tpu_custom_call" | custom-call | flops 4294967296 | bytes 4194304 | tf_op jit(solution)/shard_map/pallas_call | solution.py:182
  70.4 0.3 collective-permute-start.10
  70.6 4.7 %shard_map.72 = f32[8,256,256]{2,1,0:T(8,128)S(1)} custom-call(s32[1]{0:T(128)} %bitcast.core_ref.half_ref.owner_ref, bf16[512,2048]{1,0:T(8,128)(2,1)S(1)} %shard_map.71.f_ref, bf16[2,2048,2048]{2,1,0:T(8,128)(2,1)S(1)} %shard_map.70.bt), custom_call_target="tpu_custom_call" | custom-call | flops 4294967296 | bytes 4194304 | tf_op jit(solution)/shard_map/pallas_call | solution.py:182
  75.4 0.0 collective-permute-done.10
  75.4 1.6 %add.58 = f32[8,256,256]{2,1,0:T(8,128)} add(f32[8,256,256]{2,1,0:T(8,128)S(1)} %shard_map.72, f32[8,256,256]{2,1,0:T(8,128)S(1)} %collective-permute-done.10) | non-fusion elementwise | flops 524288 | bytes 6291456 | tf_op jit(solution)/shard_map/add | solution.py:305
  77.0 0.0 copy-start.7
  77.0 0.0 copy-start.5
  77.0 4.4 %all-to-all-start = ((f32[8,256,256]{2,1,0:T(8,128)}), f32[8,256,256]{2,1,0:T(8,128)S(1)}, u32[]{:S(2)}, u32[]{:S(2)}) async-start(f32[8,256,256]{2,1,0:T(8,128)} %add.58), calls=%async_computation | async-start | bytes 4194304 | tf_op jit(solution)/shard_map/all_to_all | solution.py:306
  81.4 0.0 copy-done.7
  81.4 0.3 collective-permute-start
  81.7 0.9 collective-permute-done.w_other_ref
  82.7 0.0 collective-permute-done.11
  82.7 30.8 %all-to-all-done.y_ref = f32[8,256,256]{2,1,0:T(8,128)S(1)} async-done(((f32[8,256,256]{2,1,0:T(8,128)}), f32[8,256,256]{2,1,0:T(8,128)S(1)}, u32[]{:S(2)}, u32[]{:S(2)}) %all-to-all-start) | async-done | bytes 2097184 | tf_op jit(solution)/shard_map/all_to_all | solution.py:306
  113.5 0.0 copy-done.5
  113.5 0.0 copy-start
  113.5 2.5 %copy-done = bf16[512,8,5,128]{3,1,2,0:T(8,128)(2,1)S(1)} copy-done((bf16[512,8,5,128]{3,1,2,0:T(8,128)(2,1)S(1)}, bf16[512,8,5,128]{3,1,2,0:T(8,128)(2,1)}, u32[]{:S(2)}) %copy-start) | copy-done | bytes 5242904
  116.0 6.3 %shard_map.74 = f32[8,5,32,128]{3,2,1,0:T(8,128)S(1)} custom-call(s32[1]{0:T(128)} %bitcast.core_ref.half_ref.owner_ref, f32[8]{0:T(128)S(1)} %broadcast_multiply_fusion.w_own_ref, f32[8]{0:T(128)S(1)} %collective-permute-done.w_other_ref, f32[8,256,256]{2,1,0:T(8,128)S(1)} %all-to-all-done.y_ref, f32[128,128]{1,0:T(8,128)S(1)} %copy-done.5, ...), custom_call_target="tpu_custom_call" | custom-call | tf_op jit(solution)/shard_map/pallas_call | solution.py:244
  122.3 15.2 %all_to_all.10 = f32[8,5,32,128]{3,2,1,0:T(8,128)S(1)} all-to-all(f32[8,5,32,128]{3,2,1,0:T(8,128)S(1)} %shard_map.74), channel_id=1, replica_groups=mesh['x'=4,'zlo'=2,'zhi'=2,'y'=4,'core'=2] {'zhi','y'}, dimensions={0} | all-to-all | bytes 1310720 | tf_op jit(solution)/shard_map/all_to_all | solution.py:308
  137.5 0.7 reduce_sum.9
  (2 shorter events, 0.0 us)
Async XLA Ops:
  0.0 37.7 %copy-start.6 = (s32[64,16]{0,1:T(8,128)S(1)}, s32[64,16]{0,1:T(8,128)}, u32[]{:S(2)}) copy-start(s32[64,16]{0,1:T(8,128)} %param.10) | copy-start | bytes 12292
  0.0 53.3 %collective-permute-start.1 = (f32[128,4096]{1,0:T(8,128)}, f32[128,4096]{1,0:T(8,128)S(1)}, u32[]{:S(2)}, u32[]{:S(2)}) collective-permute-start(f32[128,4096]{1,0:T(8,128)} %bitcast.16), channel_id=1, source_target_pairs={{0,1},{1,0},{2,3},{3,2},{4,5},{5,4},{6,7},{7,6},{8,9},{9,8},{10,11... | collective-permute-start | bytes 6291464 | tf_op jit(solution)/shard_map/ppermute | solution.py:41
  0.0 1.2 copy-start.1
  1.4 3.3 %collective-permute-start.2 = (bf16[16,64,128]{2,1,0:T(8,128)(2,1)S(1)}, bf16[16,64,128]{2,1,0:T(8,128)(2,1)S(1)}, u32[]{:S(2)}, u32[]{:S(2)}) collective-permute-start(bf16[16,64,128]{2,1,0:T(8,128)(2,1)S(1)} %shard_map.66), channel_id=1, source_target_pairs={{0,1},{1,0},{2,3},{3,2},{4,5},{5,4},{6,7},{7,6},{8,9},{9,8},{10,11... | collective-permute-start | bytes 786440 | tf_op jit(solution)/shard_map/ppermute | solution.py:41
  4.8 16.5 %collective-permute-start.3 = (bf16[2,16,64,128]{3,2,1,0:T(8,128)(2,1)S(1)}, bf16[2,16,64,128]{3,2,1,0:T(8,128)(2,1)S(1)}, u32[]{:S(2)}, u32[]{:S(2)}) collective-permute-start(bf16[2,16,64,128]{3,2,1,0:T(8,128)(2,1)S(1)} %pad_maximum_fusion.rest_0_), channel_id=1, source_target_pairs={{0,24},{1,25},{2,26},{3,27},{4,28},{5,29},{6,30},{7,31},{8,16},{9,... | collective-permute-start | bytes 1572872 | tf_op jit(solution)/shard_map/ppermute | solution.py:41
  9.0 15.0 %collective-permute-start.8 = (bf16[2,16,64,128]{3,2,1,0:T(8,128)(2,1)S(1)}, bf16[2,16,64,128]{3,2,1,0:T(8,128)(2,1)S(1)}, u32[]{:S(2)}, u32[]{:S(2)}) collective-permute-start(bf16[2,16,64,128]{3,2,1,0:T(8,128)(2,1)S(1)} %pad_maximum_fusion.rest_0_), channel_id=1, source_target_pairs={{0,2},{1,3},{2,4},{3,5},{4,6},{5,7},{6,0},{7,1},{8,10},{9,11},{10,... | collective-permute-start | bytes 1572872 | tf_op jit(solution)/shard_map/ppermute | solution.py:41
  10.6 27.1 %collective-permute-start.6 = (bf16[2,16,64,128]{3,2,1,0:T(8,128)(2,1)S(1)}, bf16[2,16,64,128]{3,2,1,0:T(8,128)(2,1)}, u32[]{:S(2)}, u32[]{:S(2)}) collective-permute-start(bf16[2,16,64,128]{3,2,1,0:T(8,128)(2,1)S(1)} %pad_maximum_fusion.rest_0_), channel_id=1, source_target_pairs={{0,4},{1,5},{2,6},{3,7},{4,0},{5,1},{6,2},{7,3},{8,12},{9,13},{10,... | collective-permute-start | bytes 1572872 | tf_op jit(solution)/shard_map/ppermute | solution.py:41
  13.5 24.3 %collective-permute-start.9 = (bf16[2,16,64,128]{3,2,1,0:T(8,128)(2,1)S(1)}, bf16[2,16,64,128]{3,2,1,0:T(8,128)(2,1)}, u32[]{:S(2)}, u32[]{:S(2)}) collective-permute-start(bf16[2,16,64,128]{3,2,1,0:T(8,128)(2,1)S(1)} %pad_maximum_fusion.rest_0_), channel_id=1, source_target_pairs={{0,6},{1,7},{2,0},{3,1},{4,2},{5,3},{6,4},{7,5},{8,14},{9,15},{10,... | collective-permute-start | bytes 1572872 | tf_op jit(solution)/shard_map/ppermute | solution.py:41
  21.3 25.7 %collective-permute-start.4 = (bf16[2,16,64,128]{3,2,1,0:T(8,128)(2,1)S(1)}, bf16[2,16,64,128]{3,2,1,0:T(8,128)(2,1)}, u32[]{:S(2)}, u32[]{:S(2)}) collective-permute-start(bf16[2,16,64,128]{3,2,1,0:T(8,128)(2,1)S(1)} %collective-permute-done.3.rest_0_), channel_id=1, source_target_pairs={{0,2},{1,3},{2,4},{3,5},{4,6},{5,7},{6,0},{7,1},{8,10},{9,11},{10,... | collective-permute-start | bytes 1572872 | tf_op jit(solution)/shard_map/ppermute | solution.py:41
  24.0 0.8 copy-start.3
  24.8 22.4 %collective-permute-start.5 = (bf16[2,16,64,128]{3,2,1,0:T(8,128)(2,1)S(1)}, bf16[2,16,64,128]{3,2,1,0:T(8,128)(2,1)}, u32[]{:S(2)}, u32[]{:S(2)}) collective-permute-start(bf16[2,16,64,128]{3,2,1,0:T(8,128)(2,1)S(1)} %collective-permute-done.3.rest_0_), channel_id=1, source_target_pairs={{0,6},{1,7},{2,0},{3,1},{4,2},{5,3},{6,4},{7,5},{8,14},{9,15},{10,... | collective-permute-start | bytes 1572872 | tf_op jit(solution)/shard_map/ppermute | solution.py:41
  37.7 13.2 %collective-permute-start.7 = (bf16[2,16,64,128]{3,2,1,0:T(8,128)(2,1)}, bf16[2,16,64,128]{3,2,1,0:T(8,128)(2,1)}, u32[]{:S(2)}, u32[]{:S(2)}) collective-permute-start(bf16[2,16,64,128]{3,2,1,0:T(8,128)(2,1)} %collective-permute-done.6.rest_0_), channel_id=1, source_target_pairs={{0,24},{1,25},{2,26},{3,27},{4,28},{5,29},{6,30},{7,31},{8,16},{9,... | collective-permute-start | bytes 1572872 | tf_op jit(solution)/shard_map/ppermute | solution.py:41
  37.8 44.9 %collective-permute-start.11 = (bf16[512,5,8,128]{3,2,1,0:T(8,128)(2,1)}, bf16[512,5,8,128]{3,2,1,0:T(8,128)(2,1)}, u32[]{:S(2)}, u32[]{:S(2)}) collective-permute-start(bf16[512,5,8,128]{3,2,1,0:T(8,128)(2,1)} %bitcast.12), channel_id=1, source_target_pairs={{0,1},{1,0},{2,3},{3,2},{4,5},{5,4},{6,7},{7,6},{8,9},{9,8},{10,11... | collective-permute-start | bytes 15728648 | tf_op jit(solution)/shard_map/ppermute | solution.py:41
  37.9 2.5 %copy-start.4 = (bf16[2,16,64,128]{3,2,1,0:T(8,128)(2,1)S(1)}, bf16[2,16,64,128]{3,2,1,0:T(8,128)(2,1)}, u32[]{:S(2)}) copy-start(bf16[2,16,64,128]{3,2,1,0:T(8,128)(2,1)} %copy-done.3) | copy-start | bytes 1572868
  43.9 9.4 %copy-start.2 = (f32[4096,8,16]{0,2,1:T(8,128)S(1)}, f32[4096,8,16]{0,2,1:T(8,128)}, u32[]{:S(2)}) copy-start(f32[4096,8,16]{0,2,1:T(8,128)} %param.6) | copy-start | bytes 6291460
  70.4 5.0 %collective-permute-start.10 = (f32[8,256,256]{2,1,0:T(8,128)S(1)}, f32[8,256,256]{2,1,0:T(8,128)S(1)}, u32[]{:S(2)}, u32[]{:S(2)}) collective-permute-start(f32[8,256,256]{2,1,0:T(8,128)S(1)} %shard_map.73), channel_id=1, source_target_pairs={{0,1},{1,0},{2,3},{3,2},{4,5},{5,4},{6,7},{7,6},{8,9},{9,8},{10,11... | collective-permute-start | bytes 6291464 | tf_op jit(solution)/shard_map/ppermute | solution.py:41
  77.0 4.4 %copy-start.7 = (f32[8]{0:T(128)S(1)}, f32[8]{0:T(128)}, u32[]{:S(2)}) copy-start(f32[8]{0:T(128)} %param.8) | copy-start | bytes 100
  77.0 36.5 %copy-start.5 = (f32[128,128]{1,0:T(8,128)S(1)}, f32[128,128]{1,0:T(8,128)}, u32[]{:S(2)}) copy-start(f32[128,128]{1,0:T(8,128)} %v_ref.1) | copy-start | bytes 196612
  77.0 36.5 %all-to-all-start = ((f32[8,256,256]{2,1,0:T(8,128)}), f32[8,256,256]{2,1,0:T(8,128)S(1)}, u32[]{:S(2)}, u32[]{:S(2)}) async-start(f32[8,256,256]{2,1,0:T(8,128)} %add.58), calls=%async_computation | async-start | bytes 4194304 | tf_op jit(solution)/shard_map/all_to_all | solution.py:306
  81.4 1.2 collective-permute-start
  113.5 2.5 %copy-start = (bf16[512,8,5,128]{3,1,2,0:T(8,128)(2,1)S(1)}, bf16[512,8,5,128]{3,1,2,0:T(8,128)(2,1)}, u32[]{:S(2)}) copy-start(bf16[512,8,5,128]{3,1,2,0:T(8,128)(2,1)} %param.7) | copy-start | bytes 15728644
where the time goes:
time: 139 us; the launch traced here: 138 us
  waiting for transfers between devices  58.9 us (42%)
  Pallas kernels  36.7 us (26%)
  starting transfers between devices  20.2 us (15%)
  blocking collectives  15.2 us (11%)
  local copies, waits for them, and re-layouts  4.66 us (3%)
  other arithmetic  2.37 us (2%)
    all_to_all x1, waiting for transfers between devices, shards(): y = lax.all_to_all(y, ('x', 'zlo'), split_axis=0, concat_axis=0, tiled=True)  30.8 us
    ppermute x12, waiting for transfers between devices, send(): return lax.ppermute(value, AXES, pairs)  28.1 us
    ppermute x12, starting transfers between devices, send(): return lax.ppermute(value, AXES, pairs)  15.8 us
    all_to_all x1, blocking collectives, shards(): lax.all_to_all(out, ('zhi', 'y'), split_axis=0, concat_axis=0, tiled=True)  15.2 us
    pallas_call x2, Pallas kernels, backward_call(): pl.pallas_call(backward_kernel, out_shape=jax.ShapeDtypeStruct((groups, f...  9.45 us
    pallas_call x1, Pallas kernels, forward_call(): pl.pallas_call(forward_kernel, out_shape=jax.ShapeDtypeStruct((x.shape[1]...  9.03 us
    pallas_call x4, Pallas kernels, place_call(): pl.pallas_call(functools.partial(place_kernel, slots), out_shape=jax.Shap...  8.25 us
    pallas_call x1, Pallas kernels, post_call(): pl.pallas_call(post_kernel, grid_spec=grid_spec, out_shape=jax.ShapeDtype...  6.32 us
  transfers between devices with their start and end apart: 13, of which 9 were waited for; matrix products, arithmetic and copies ran while one was open for 1% of the time, Pallas kernels for 22%

commit v1 on v0

--- a/solution.py
+++ b/solution.py
@@ -31,6 +31,7 @@
 Y_UP = perm(lambda x, y, z, c: (x, y + 1, z, c))
 Y_DOWN = perm(lambda x, y, z, c: (x, y - 1, z, c))
 Y_FAR = perm(lambda x, y, z, c: (x, y + 2, z, c))
+X_PAIR = perm(lambda x, y, z, c: (x ^ 1, y, z, c))
 CORE = perm(lambda x, y, z, c: (x, y, z, 1 - c))
 LIMIT = 20 * 1024 * 1024
 VMEM = pl.BlockSpec(memory_space=pltpu.VMEM)
@@ -63,6 +64,30 @@
         out_specs=VMEM,
         compiler_params=pltpu.CompilerParams(vmem_limit_bytes=LIMIT),
     )(half, b)
+
+
+def assemble_kernel(odd_ref, keep_ref, handed_ref, unit_ref, first_ref, second_ref, far_ref):
+    half = first_ref.shape[1]
+    for slot, ref in enumerate((keep_ref, handed_ref)):
+        unit_ref[slot] = ref[...]
+        first_ref[slot] = ref[:half]
+        second_ref[slot] = ref[half:]
+
+        @pl.when(odd_ref[0] == slot)
+        def _(ref=ref):
+            far_ref[0] = ref[...]
+
+
+def assemble(odd, keep, handed):
+    rows, q, p = keep.shape
+    counts = ((2, rows), (2, rows // 2), (2, rows // 2), (1, rows))
+    return pl.pallas_call(
+        assemble_kernel,
+        out_shape=tuple(jax.ShapeDtypeStruct(c + (q, p), BF) for c in counts),
+        in_specs=[SMEM, VMEM, VMEM],
+        out_specs=(VMEM,) * 4,
+        compiler_params=pltpu.CompilerParams(vmem_limit_bytes=LIMIT),
+    )(odd, keep, handed)
 
 
 def prep_kernel(core_ref, own_ref, other_ref, o_ref):
@@ -91,11 +116,11 @@
     )(core, own, other)
 
 
-def place_kernel(slots, cols_ref, core_ref, jtab_ref, *rest):
-    pieces, bt = rest[: len(slots)], rest[-1]
+def place_kernel(plan, zero_first, cols_ref, core_ref, jtab_ref, *rest):
+    pieces, bt = rest[: len(plan)], rest[-1]
     n_half, lanes = bt.shape[1:]
     first = core_ref[0] * (cols_ref.shape[0] // 2)
-    if len(rest) == len(slots) + 1:
+    if zero_first:
 
         def zero(r, _):
             s = pl.ds(pl.multiple_of(r * 64, 64), 64)
@@ -104,57 +129,56 @@
             return 0
 
         lax.fori_loop(0, n_half // 64, zero, 0)
-    for piece, slot in zip(pieces, slots):
+    for piece, (slot, start) in zip(pieces, plan):
         for s in range(piece.shape[0]):
             j = jtab_ref[slot + s]
             for t in range(piece.shape[1]):
                 tile = piece[s, t]
                 for h in range(2):
-                    row = pl.multiple_of(cols_ref[first + 2 * t + h, j] * 32, 32)
-                    lane = t * 128 + h * 64
+                    i = 2 * (start + t) + h
+                    row = pl.multiple_of(cols_ref[first + i, j] * 32, 32)
                     for owner in range(2):
                         part = tile[owner * 32 : owner * 32 + 32, h * 64 : h * 64 + 64]
-                        bt[owner, pl.ds(row, 32), lane : lane + 64] = part
-
-
-def place_call(cols, core, jtab, pieces, slots, shape, dense=None):
+                        bt[owner, pl.ds(row, 32), i * 64 : i * 64 + 64] = part
+
+
+def place_call(cols, core, jtab, pieces, plan, shape, dense=None, after=()):
     given = () if dense is None else (dense,)
-    position = 3 + len(pieces)
-    return pl.pallas_call(
-        functools.partial(place_kernel, slots),
+    position = 3 + len(pieces) + len(after)
+    return pl.pallas_call(
+        functools.partial(place_kernel, plan, dense is None),
         out_shape=jax.ShapeDtypeStruct(shape, BF),
-        in_specs=[SMEM] * 3 + [VMEM] * (len(pieces) + len(given)),
+        in_specs=[SMEM] * 3
+        + [VMEM] * len(pieces)
+        + [pl.BlockSpec(memory_space=pl.ANY)] * len(after)
+        + [VMEM] * len(given),
         out_specs=VMEM,
         input_output_aliases={position: 0} if given else {},
         compiler_params=pltpu.CompilerParams(vmem_limit_bytes=LIMIT),
-    )(cols, core, jtab, *pieces, *given)
-
-
-def forward_kernel(x_ref, bt, f_ref):
+    )(cols, core, jtab, *pieces, *after, *given)
+
+
+def forward_kernel(begin, x_ref, bt, f_ref):
     columns = x_ref.shape[1] // 2
-    width = 1024
-
-    def step(n, _):
-        s = pl.ds(pl.multiple_of(n * width, width), width)
-        f = jnp.dot(x_ref[0], bt[0, :, s], preferred_element_type=F32)
-        f += jnp.dot(x_ref[1], bt[1, :, s], preferred_element_type=F32)
-        hi, lo = split2(f[:columns] + f[columns:])
-        f_ref[0:columns, s] = hi
-        f_ref[columns:, s] = lo
-        return 0
-
-    lax.fori_loop(0, bt.shape[2] // width, step, 0)
-
-
-def backward_kernel(owner_ref, f_ref, bt, o_ref):
+    s = slice(begin, begin + f_ref.shape[1])
+    f = jnp.dot(x_ref[0], bt[0, :, s], preferred_element_type=F32)
+    f += jnp.dot(x_ref[1], bt[1, :, s], preferred_element_type=F32)
+    hi, lo = split2(f[:columns] + f[columns:])
+    f_ref[0:columns] = hi
+    f_ref[columns:] = lo
+
+
+def backward_kernel(owner_ref, fa_ref, fb_ref, bt, o_ref):
     groups, columns, width = o_ref.shape
     per = 4
+    cut = fa_ref.shape[1]
+    dims = (((1,), (1,)), ((), ()))
 
     def step(n, _):
         s = pl.ds(pl.multiple_of(n * per * width, per * width), per * width)
-        y = lax.dot_general(
-            f_ref[...], bt[owner_ref[0], s], (((1,), (1,)), ((), ())), preferred_element_type=F32
-        )
+        rows = bt.at[owner_ref[0], s]
+        y = lax.dot_general(fa_ref[...], rows[:, :cut], dims, preferred_element_type=F32)
+        y += lax.dot_general(fb_ref[...], rows[:, cut:], dims, preferred_element_type=F32)
         y = y[:columns] + y[columns:]
         for g in range(per):
             o_ref[per * n + g] = y[:, g * width : (g + 1) * width]
@@ -163,11 +187,11 @@
     lax.fori_loop(0, groups // per, step, 0)
 
 
-def forward_call(x, dense):
-    lanes = dense.shape[2]
+def forward_call(x, dense, begin):
+    lanes = dense.shape[2] // 2
     flops = 4 * x.shape[1] * x.shape[2] * lanes
     return pl.pallas_call(
-        forward_kernel,
+        functools.partial(forward_kernel, begin),
         out_shape=jax.ShapeDtypeStruct((x.shape[1], lanes), BF),
         in_specs=[VMEM, VMEM],
         out_specs=VMEM,
@@ -176,17 +200,17 @@
     )(x, dense)
 
 
-def backward_call(owner, f, dense, groups):
+def backward_call(owner, fa, fb, dense, groups):
     n_half, lanes = dense.shape[1:]
-    flops = 2 * f.shape[0] * n_half * lanes
+    flops = 2 * fa.shape[0] * n_half * lanes
     return pl.pallas_call(
         backward_kernel,
-        out_shape=jax.ShapeDtypeStruct((groups, f.shape[0] // 2, n_half // groups), F32),
-        in_specs=[SMEM, VMEM, VMEM],
+        out_shape=jax.ShapeDtypeStruct((groups, fa.shape[0] // 2, n_half // groups), F32),
+        in_specs=[SMEM, VMEM, VMEM, VMEM],
         out_specs=VMEM,
         compiler_params=pltpu.CompilerParams(vmem_limit_bytes=LIMIT),
         cost_estimate=pl.CostEstimate(flops=flops, bytes_accessed=4 << 20, transcendentals=0),
-    )(owner, f, dense)
+    )(owner, fa, fb, dense)
 
 
 def post_kernel(core_ref, w_own_ref, w_other_ref, y_ref, v_ref, own_ref, other_ref, o_ref, loc):
@@ -249,28 +273,50 @@
     )(core, w_own, w_other, y, v, own, other)
 
 
-LAYOUT = ((0, 0), (0, 1), (3, 0), (1, 0), (2, 0), (3, 1), (1, 1), (2, 1))
-
-
-STAGES = ((0,), (1, 2, 3), (4,), (5, 6, 7))
-
-
-def gather(unit):
-    near = send(unit, Z_NEAR)
+SLOTS = (
+    [(0, 0, c, 0) for c in (0, 1)]
+    + [(0, 1, c, 0) for c in (0, 1)]
+    + [(3, 0, c, 0) for c in (0, 1)]
+    + [(1, 0, c, 0) for c in (0, 1)]
+    + [(2, 0, 0, 1), (2, 0, 1, 1), (2, 1, 0, 1), (2, 1, 1, 1)]
+    + [(3, 1, c, 0) for c in (0, 1)]
+    + [(1, 1, c, 0) for c in (0, 1)]
+)
+
+
+def gather(keep, handed):
+    half = keep.shape[0] // 2
+    odd = (lax.axis_index("x") % 2).reshape(1).astype(jnp.int32)
+    unit, first, second, chosen = assemble(odd, keep, handed)
+    near_a = send(first, Z_NEAR)
+    near_b = send(second, Z_NEAR)
+    far_a = send(chosen, Y_FAR)
     up = send(unit, Y_UP)
     down = send(unit, Y_DOWN)
-    far = send(unit, Y_FAR)
-    near_up = send(near, Y_UP)
-    near_down = send(near, Y_DOWN)
-    near_far = send(far, Z_NEAR)
-    return [unit, near, up, down, far, near_up, near_down, near_far]
+    far_b = send(far_a, X_PAIR)
+    near_far_a = send(far_a, Z_NEAR)
+    up_a = send(near_a, Y_UP)
+    down_a = send(near_a, Y_DOWN)
+    near_far_b = send(far_b, Z_NEAR)
+    up_b = send(near_b, Y_UP)
+    down_b = send(near_b, Y_DOWN)
+    return (
+        ((unit, 0, 0),),
+        ((near_a, 2, 0), (near_b, 2, half), (far_a, 8, 0), (far_b, 9, 0)),
+        ((up, 4, 0), (down, 6, 0)),
+        ((near_far_a, 10, 0), (near_far_b, 11, 0)),
+        ((up_a, 12, 0), (down_a, 14, 0)),
+        ((up_b, 12, half), (down_b, 14, half)),
+    )
 
 
 def slot_table():
     zhi, y, c = lax.axis_index("zhi"), lax.axis_index("y"), lax.axis_index("core")
-    slot = jnp.arange(16, dtype=jnp.int32)
-    dy, dz = (sum(jnp.where(slot // 2 == i, d[n], 0) for i, d in enumerate(LAYOUT)) for n in (0, 1))
-    return ((zhi ^ dz) * 8 + ((y + dy) & 3) * 2 + (c ^ (slot & 1))).astype(jnp.int32)
+    odd = lax.axis_index("x") & 1
+    slot = jnp.arange(len(SLOTS), dtype=jnp.int32)
+    picks = (sum(jnp.where(slot == i, d[n], 0) for i, d in enumerate(SLOTS)) for n in range(4))
+    dy, dz, dc, dx = picks
+    return ((zhi ^ dz) * 8 + ((y + dy) & 3) * 2 + (c ^ dc ^ (dx & odd))).astype(jnp.int32)
 
 
 def shards(control, perturb, member_weights, blocks, block_cols, vertical):
@@ -282,7 +328,7 @@
     other = 1 - core
     stored = blocks[:, 0]
     handed = send(pack(other, stored), CORE)
-    pieces = gather(jnp.stack([pack(core, stored), handed]))
+    stages = gather(pack(core, stored), handed)
     x = control.transpose(1, 2, 0).reshape(mem_dev * lev_dev, nodes_all)
     x_other = send(x, CORE)
     xc = prep_call(core, x, x_other)
@@ -294,14 +340,15 @@
     fields, fields_other = fields.reshape(shape), fields_other.reshape(shape)
     table = slot_table()
     shape = (2, nodes_all // 2, nodes_all // 2)
-    dense = None
-    for part in STAGES:
-        slots = tuple(2 * p for p in part)
-        some = [pieces[p] for p in part]
-        dense = place_call(block_cols, core, table, some, slots, shape, dense)
-    f = forward_call(xc, dense)
-    give = backward_call(other, f, dense, groups)
-    keep = backward_call(core, f, dense, groups)
+    dense, halves = None, ()
+    for stage, parts in enumerate(stages):
+        pieces, plan = [p[0] for p in parts], tuple(p[1:] for p in parts)
+        args = (block_cols, core, table, pieces, plan, shape)
+        dense = place_call(*args, dense, halves)
+        if stage >= len(stages) - 2:
+            halves += (forward_call(xc, dense, len(halves) * shape[2] // 2),)
+    give = backward_call(other, *halves, dense, groups)
+    keep = backward_call(core, *halves, dense, groups)
     y = keep + send(give, CORE)
     y = lax.all_to_all(y, ("x", "zlo"), split_axis=0, concat_axis=0, tiled=True)
     out = post_call(core, weights, weights_other, y, vertical, fields, fields_other)

time: 139 us -> 139 us (level)
  waiting for transfers between devices: 58.9 us -> 38.7 us
  starting transfers between devices: 20.2 us -> 32.2 us
  blocking collectives: 15.2 us -> 18.6 us
  local copies, waits for them, and re-layouts: 4.66 us -> 7.56 us
  Pallas kernels: 36.7 us -> 38.6 us
    ppermute x12 -> x17, waiting for transfers between devices: 28.1 us -> 8.09 us  [send(): return lax.ppermute(value, AXES, pairs)]
    ppermute x12 -> x17, starting transfers between devices: 15.8 us -> 27.9 us  [send(): return lax.ppermute(value, AXES, pairs)]
    all_to_all x1, blocking collectives: 15.2 us -> 18.6 us  [shards(): lax.all_to_all(out, ('zhi', 'y'), split_axis=0, concat_axis=0, tiled=True)]
    unnamed x17, local copies, waits for them, and re-layouts: 4.66 us -> 7.56 us
    pallas_call x5 -> x9, Pallas kernels: 17.3 us -> 19.2 us  [the longest x6 10.1 us: place_call(): pl.pallas_call(functools.partial(place_kernel, plan, dense is None), out_...]
  transfers between devices with their start and end apart: 13 -> 18, of which waited for: 9 -> 5; matrix products, arithmetic and copies ran while one was open for 1% -> 2% of each run, Pallas kernels for 22% -> 23%
where the time goes in v1:
time: 139 us; the launch traced here: 138 us
  waiting for transfers between devices  38.7 us (28%)
  Pallas kernels  38.6 us (28%)
  starting transfers between devices  32.2 us (23%)
  blocking collectives  18.6 us (13%)
  local copies, waits for them, and re-layouts  7.56 us (5%)
  other arithmetic  2.31 us (2%)
    all_to_all x1, waiting for transfers between devices, shards(): y = lax.all_to_all(y, ('x', 'zlo'), split_axis=0, concat_axis=0, tiled=True)  30.6 us
    ppermute x17, starting transfers between devices, send(): return lax.ppermute(value, AXES, pairs)  27.9 us
    all_to_all x1, blocking collectives, shards(): lax.all_to_all(out, ('zhi', 'y'), split_axis=0, concat_axis=0, tiled=True)  18.6 us
    pallas_call x6, Pallas kernels, place_call(): pl.pallas_call(functools.partial(place_kernel, plan, dense is None), out_...  10.1 us
    pallas_call x2, Pallas kernels, backward_call(): pl.pallas_call(backward_kernel, out_shape=jax.ShapeDtypeStruct((groups, f...  9.45 us
    pallas_call x2, Pallas kernels, forward_call(): pl.pallas_call(functools.partial(forward_kernel, begin), out_shape=jax.Sh...  8.97 us
    ppermute x17, waiting for transfers between devices, send(): return lax.ppermute(value, AXES, pairs)  8.09 us
    unnamed x17, local copies, waits for them, and re-layouts  7.56 us
  transfers between devices with their start and end apart: 18, of which 5 were waited for; matrix products, arithmetic and copies ran while one was open for 2% of the time, Pallas kernels for 23%

profile of v1, /device:TPU:0, one launch (start us, length us, event | category | flops | bytes accessed | tf_op | source)
XLA Modules:
  0.0 138.2 jit_solution(7460126919754469634)
XLA Ops:
  0.0 0.0 collective-permute-start.1
  0.0 1.2 copy-done.1
  1.2 0.2 shard_map.66
  1.4 0.6 collective-permute-start.2
  2.0 1.2 copy-done.2
  3.2 0.2 shard_map.65.keep_ref
  3.4 1.3 collective-permute-done.2.handed_ref
  4.7 0.2 shard_map.67
  4.9 3.4 %collective-permute-start.6 = (bf16[1,16,64,128]{3,2,1,0:T(8,128)(2,1)S(1)}, bf16[1,16,64,128]{3,2,1,0:T(8,128)(2,1)}, u32[]{:S(2)}, u32[]{:S(2)}) collective-permute-start(bf16[1,16,64,128]{3,2,1,0:T(8,128)(2,1)S(1)} %get-tuple-element.10), channel_id=1, source_target_pairs={{0,4},{1,5},{2,6},{3,7},{4,0},{5,1},{6,2},{7,3},{8,12},{9,13},{10,... | collective-permute-start | bytes 786440 | tf_op jit(solution)/shard_map/ppermute | solution.py:42
  8.3 4.0 %collective-permute-start.12 = (bf16[2,8,64,128]{3,2,1,0:T(8,128)(2,1)S(1)}, bf16[2,8,64,128]{3,2,1,0:T(8,128)(2,1)S(1)}, u32[]{:S(2)}, u32[]{:S(2)}) collective-permute-start(bf16[2,8,64,128]{3,2,1,0:T(8,128)(2,1)S(1)} %get-tuple-element.12), channel_id=1, source_target_pairs={{0,24},{1,25},{2,26},{3,27},{4,28},{5,29},{6,30},{7,31},{8,16},{9,... | collective-permute-start | bytes 786440 | tf_op jit(solution)/shard_map/ppermute | solution.py:42
  12.3 0.7 collective-permute-start.10
  13.0 2.6 %collective-permute-start.11 = (bf16[2,16,64,128]{3,2,1,0:T(8,128)(2,1)S(1)}, bf16[2,16,64,128]{3,2,1,0:T(8,128)(2,1)S(1)}, u32[]{:S(2)}, u32[]{:S(2)}) collective-permute-start(bf16[2,16,64,128]{3,2,1,0:T(8,128)(2,1)S(1)} %get-tuple-element.11.rest_0_), channel_id=1, source_target_pairs={{0,6},{1,7},{2,0},{3,1},{4,2},{5,3},{6,4},{7,5},{8,14},{9,15},{10,... | collective-permute-start | bytes 1572872 | tf_op jit(solution)/shard_map/ppermute | solution.py:42
  15.6 0.8 copy-done.4
  16.4 0.0 collective-permute-done.6.rest_2_
  16.4 3.6 %collective-permute-start.3 = (bf16[2,8,64,128]{3,2,1,0:T(8,128)(2,1)S(1)}, bf16[2,8,64,128]{3,2,1,0:T(8,128)(2,1)}, u32[]{:S(2)}, u32[]{:S(2)}) collective-permute-start(bf16[2,8,64,128]{3,2,1,0:T(8,128)(2,1)S(1)} %get-tuple-element.9), channel_id=1, source_target_pairs={{0,24},{1,25},{2,26},{3,27},{4,28},{5,29},{6,30},{7,31},{8,16},{9,... | collective-permute-start | bytes 786440 | tf_op jit(solution)/shard_map/ppermute | solution.py:42
  20.0 0.0 collective-permute-done.12.rest_1_
  20.0 1.5 %collective-permute-start.8 = (bf16[1,16,64,128]{3,2,1,0:T(8,128)(2,1)}, bf16[1,16,64,128]{3,2,1,0:T(8,128)(2,1)}, u32[]{:S(2)}, u32[]{:S(2)}) collective-permute-start(bf16[1,16,64,128]{3,2,1,0:T(8,128)(2,1)} %collective-permute-done.6.rest_2_), channel_id=1, source_target_pairs={{0,32},{1,33},{2,34},{3,35},{4,36},{5,37},{6,38},{7,39},{8,40},{9,... | collective-permute-start | bytes 786440 | tf_op jit(solution)/shard_map/ppermute | solution.py:42
  21.5 3.5 %collective-permute-done.3.rest_0_ = bf16[2,8,64,128]{3,2,1,0:T(8,128)(2,1)} collective-permute-done((bf16[2,8,64,128]{3,2,1,0:T(8,128)(2,1)S(1)}, bf16[2,8,64,128]{3,2,1,0:T(8,128)(2,1)}, u32[]{:S(2)}, u32[]{:S(2)}) %collective-permute-start.3) | collective-permute-done | bytes 262176 | tf_op jit(solution)/shard_map/ppermute | solution.py:42
  25.0 3.0 %collective-permute-start.7 = (bf16[1,16,64,128]{3,2,1,0:T(8,128)(2,1)}, bf16[1,16,64,128]{3,2,1,0:T(8,128)(2,1)}, u32[]{:S(2)}, u32[]{:S(2)}) collective-permute-start(bf16[1,16,64,128]{3,2,1,0:T(8,128)(2,1)} %collective-permute-done.6.rest_2_), channel_id=1, source_target_pairs={{0,24},{1,25},{2,26},{3,27},{4,28},{5,29},{6,30},{7,31},{8,16},{9,... | collective-permute-start | bytes 786440 | tf_op jit(solution)/shard_map/ppermute | solution.py:42
  27.9 0.0 collective-permute-done.8.rest_3_
  28.0 1.2 collective-permute-start.9
  29.1 0.0 collective-permute-done.10.rest_0_
  29.1 0.7 collective-permute-start.4
  29.8 0.0 collective-permute-done.11.rest_1_
  29.8 2.6 %collective-permute-start.5 = (bf16[2,8,64,128]{3,2,1,0:T(8,128)(2,1)}, bf16[2,8,64,128]{3,2,1,0:T(8,128)(2,1)}, u32[]{:S(2)}, u32[]{:S(2)}) collective-permute-start(bf16[2,8,64,128]{3,2,1,0:T(8,128)(2,1)} %collective-permute-done.3.rest_0_), channel_id=1, source_target_pairs={{0,6},{1,7},{2,0},{3,1},{4,2},{5,3},{6,4},{7,5},{8,14},{9,15},{10,... | collective-permute-start | bytes 786440 | tf_op jit(solution)/shard_map/ppermute | solution.py:42
  32.4 0.8 copy.16.cols_ref
  33.2 2.3 %collective-permute-done.7.rest_0_ = bf16[1,16,64,128]{3,2,1,0:T(8,128)(2,1)} collective-permute-done((bf16[1,16,64,128]{3,2,1,0:T(8,128)(2,1)}, bf16[1,16,64,128]{3,2,1,0:T(8,128)(2,1)}, u32[]{:S(2)}, u32[]{:S(2)}) %collective-permute-start.7) | collective-permute-done | bytes 262176 | tf_op jit(solution)/shard_map/ppermute | solution.py:42
  35.4 0.0 collective-permute-start.16
  35.5 1.0 copy-done.5
  36.5 2.5 %shard_map.68.rest_4_ = bf16[2,2048,2048]{2,1,0:T(8,128)(2,1)S(1)} custom-call(s32[64,16]{1,0:T(8,128)S(1)} %copy.16.cols_ref, s32[1]{0:T(128)} %bitcast.core_ref.half_ref.owner_ref, s32[16]{0:T(128)S(1)} %xor_add_fusion.jtab_ref, bf16[2,16,64,128]{3,2,1,0:T(8,128)(2,1)S(1)} %copy-done.5), custom_call_target="tpu_custom_call" | custom-call | tf_op jit(solution)/shard_map/pallas_call | solution.py:148
  39.0 1.7 %shard_map.69.rest_2_ = bf16[2,2048,2048]{2,1,0:T(8,128)(2,1)S(1)} custom-call(s32[64,16]{1,0:T(8,128)S(1)} %copy.16.cols_ref, s32[1]{0:T(128)} %bitcast.core_ref.half_ref.owner_ref, s32[16]{0:T(128)S(1)} %xor_add_fusion.jtab_ref, bf16[2,8,64,128]{3,2,1,0:T(8,128)(2,1)} %collective-permute-done.3.rest_0_, ...), custom_call_target="tpu_custom_call", output_to_operand_aliasing={{}: (7, {})} | custom-call | tf_op jit(solution)/shard_map/pallas_call | solution.py:148
  40.7 1.7 %shard_map.70.rest_2_ = bf16[2,2048,2048]{2,1,0:T(8,128)(2,1)S(1)} custom-call(s32[64,16]{1,0:T(8,128)S(1)} %copy.16.cols_ref, s32[1]{0:T(128)} %bitcast.core_ref.half_ref.owner_ref, s32[16]{0:T(128)S(1)} %xor_add_fusion.jtab_ref, bf16[2,16,64,128]{3,2,1,0:T(8,128)(2,1)S(1)} %collective-permute-done.10.rest_0_, ...), custom_call_target="tpu_custom_call", output_to_operand_aliasing={{}: (5, {})} | custom-call | tf_op jit(solution)/shard_map/pallas_call | solution.py:148
  42.4 0.0 collective-permute-done.9.rest_1_
  42.5 1.6 %collective-permute-start.13 = (bf16[2,8,64,128]{3,2,1,0:T(8,128)(2,1)S(1)}, bf16[2,8,64,128]{3,2,1,0:T(8,128)(2,1)S(1)}, u32[]{:S(2)}, u32[]{:S(2)}) collective-permute-start(bf16[2,8,64,128]{3,2,1,0:T(8,128)(2,1)S(1)} %collective-permute-done.12.rest_1_), channel_id=1, source_target_pairs={{0,2},{1,3},{2,4},{3,5},{4,6},{5,7},{6,0},{7,1},{8,10},{9,11},{10,... | collective-permute-start | bytes 786440 | tf_op jit(solution)/shard_map/ppermute | solution.py:42
  44.1 1.3 shard_map.71.rest_2_
  45.4 0.0 copy-start.3
  45.4 0.0 collective-permute-done.4.rest_0_
  45.4 1.9 %collective-permute-start.14 = (bf16[2,8,64,128]{3,2,1,0:T(8,128)(2,1)S(1)}, bf16[2,8,64,128]{3,2,1,0:T(8,128)(2,1)S(1)}, u32[]{:S(2)}, u32[]{:S(2)}) collective-permute-start(bf16[2,8,64,128]{3,2,1,0:T(8,128)(2,1)S(1)} %collective-permute-done.12.rest_1_), channel_id=1, source_target_pairs={{0,6},{1,7},{2,0},{3,1},{4,2},{5,3},{6,4},{7,5},{8,14},{9,15},{10,... | collective-permute-start | bytes 786440 | tf_op jit(solution)/shard_map/ppermute | solution.py:42
  47.4 0.0 collective-permute-done.5.rest_1_
  47.4 1.4 %shard_map.72.bt.rest_3_ = bf16[2,2048,2048]{2,1,0:T(8,128)(2,1)S(1)} custom-call(s32[64,16]{1,0:T(8,128)S(1)} %copy.16.cols_ref, s32[1]{0:T(128)} %bitcast.core_ref.half_ref.owner_ref, s32[16]{0:T(128)S(1)} %xor_add_fusion.jtab_ref, bf16[2,8,64,128]{3,2,1,0:T(8,128)(2,1)} %collective-permute-done.4.rest_0_, ...), custom_call_target="tpu_custom_call", output_to_operand_aliasing={{}: (5, {})} | custom-call | tf_op jit(solution)/shard_map/pallas_call | solution.py:148
  48.8 0.0 collective-permute-done.1.other_ref
  48.8 0.0 copy-done.3
  48.8 3.3 %shard_map.64.x_ref = bf16[2,512,2048]{2,1,0:T(8,128)(2,1)S(1)} custom-call(s32[1]{0:T(128)} %bitcast.core_ref.half_ref.owner_ref, f32[128,4096]{1,0:T(8,128)S(1)} %bitcast.16, f32[128,4096]{1,0:T(8,128)S(1)} %collective-permute-done.1.other_ref), custom_call_target="tpu_custom_call" | custom-call | tf_op jit(solution)/shard_map/pallas_call | solution.py:109
  52.1 4.5 %shard_map.73.rest_2_.fa_ref = bf16[512,1024]{1,0:T(8,128)(2,1)S(1)} custom-call(bf16[2,512,2048]{2,1,0:T(8,128)(2,1)S(1)} %shard_map.64.x_ref, bf16[2,2048,2048]{2,1,0:T(8,128)(2,1)S(1)} %shard_map.72.bt.rest_3_), custom_call_target="tpu_custom_call" | custom-call | flops 4294967296 | bytes 8388608 | tf_op jit(solution)/shard_map/pallas_call | solution.py:193
  56.6 0.0 collective-permute-done.13.rest_0_
  56.6 0.0 collective-permute-done.14.rest_1_
  56.6 1.4 %shard_map.74.bt = bf16[2,2048,2048]{2,1,0:T(8,128)(2,1)S(1)} custom-call(s32[64,16]{1,0:T(8,128)S(1)} %copy.16.cols_ref, s32[1]{0:T(128)} %bitcast.core_ref.half_ref.owner_ref, s32[16]{0:T(128)S(1)} %xor_add_fusion.jtab_ref, bf16[2,8,64,128]{3,2,1,0:T(8,128)(2,1)S(1)} %collective-permute-done.13.rest_0_, ...), custom_call_target="tpu_custom_call", output_to_operand_aliasing={{}: (6, {})} | custom-call | tf_op jit(solution)/shard_map/pallas_call | solution.py:148
  58.0 4.5 %shard_map.75.fb_ref = bf16[512,1024]{1,0:T(8,128)(2,1)S(1)} custom-call(bf16[2,512,2048]{2,1,0:T(8,128)(2,1)S(1)} %shard_map.64.x_ref, bf16[2,2048,2048]{2,1,0:T(8,128)(2,1)S(1)} %shard_map.74.bt), custom_call_target="tpu_custom_call" | custom-call | flops 4294967296 | bytes 8388608 | tf_op jit(solution)/shard_map/pallas_call | solution.py:193
  62.5 4.7 %shard_map.77 = f32[8,256,256]{2,1,0:T(8,128)S(1)} custom-call(s32[1]{0:T(128)S(6)} %sub.3.half_ref.owner_ref, bf16[512,1024]{1,0:T(8,128)(2,1)S(1)} %shard_map.73.rest_2_.fa_ref, bf16[512,1024]{1,0:T(8,128)(2,1)S(1)} %shard_map.75.fb_ref, bf16[2,2048,2048]{2,1,0:T(8,128)(2,1)S(1)} %shard_map.74.bt), custom_call_target="tpu_custom_call" | custom-call | flops 4294967296 | bytes 4194304 | tf_op jit(solution)/shard_map/pallas_call | solution.py:206
  67.3 0.1 collective-permute-start.15
  67.4 4.7 %shard_map.76 = f32[8,256,256]{2,1,0:T(8,128)S(1)} custom-call(s32[1]{0:T(128)} %bitcast.core_ref.half_ref.owner_ref, bf16[512,1024]{1,0:T(8,128)(2,1)S(1)} %shard_map.73.rest_2_.fa_ref, bf16[512,1024]{1,0:T(8,128)(2,1)S(1)} %shard_map.75.fb_ref, bf16[2,2048,2048]{2,1,0:T(8,128)(2,1)S(1)} %shard_map.74.bt), custom_call_target="tpu_custom_call" | custom-call | flops 4294967296 | bytes 4194304 | tf_op jit(solution)/shard_map/pallas_call | solution.py:206
  72.1 0.0 copy-start.7
  72.1 0.0 copy-start.6
  72.1 0.0 collective-permute-done.15
  72.1 1.6 %add.168 = f32[8,256,256]{2,1,0:T(8,128)} add(f32[8,256,256]{2,1,0:T(8,128)S(1)} %shard_map.76, f32[8,256,256]{2,1,0:T(8,128)S(1)} %collective-permute-done.15) | non-fusion elementwise | flops 524288 | bytes 6291456 | tf_op jit(solution)/shard_map/add | solution.py:352
  73.7 4.3 %all-to-all-start = ((f32[8,256,256]{2,1,0:T(8,128)}), f32[8,256,256]{2,1,0:T(8,128)S(1)}, u32[]{:S(2)}, u32[]{:S(2)}) async-start(f32[8,256,256]{2,1,0:T(8,128)} %add.168), calls=%async_computation | async-start | bytes 4194304 | tf_op jit(solution)/shard_map/all_to_all | solution.py:353
  78.1 0.5 collective-permute-start
  78.6 1.0 collective-permute-done.w_other_ref
  79.5 0.0 collective-permute-done.16
  79.5 30.6 %all-to-all-done.y_ref = f32[8,256,256]{2,1,0:T(8,128)S(1)} async-done(((f32[8,256,256]{2,1,0:T(8,128)}), f32[8,256,256]{2,1,0:T(8,128)S(1)}, u32[]{:S(2)}, u32[]{:S(2)}) %all-to-all-start) | async-done | bytes 2097184 | tf_op jit(solution)/shard_map/all_to_all | solution.py:353
  110.1 2.5 %copy-done = bf16[512,8,5,128]{3,1,2,0:T(8,128)(2,1)S(1)} copy-done((bf16[512,8,5,128]{3,1,2,0:T(8,128)(2,1)S(1)}, bf16[512,8,5,128]{3,1,2,0:T(8,128)(2,1)}, u32[]{:S(2)}) %copy-start) | copy-done | bytes 5242904
  112.6 6.3 %shard_map.78 = f32[8,5,32,128]{3,2,1,0:T(8,128)S(1)} custom-call(s32[1]{0:T(128)} %bitcast.core_ref.half_ref.owner_ref, f32[8]{0:T(128)S(1)} %broadcast_multiply_fusion.w_own_ref, f32[8]{0:T(128)S(1)} %collective-permute-done.w_other_ref, f32[8,256,256]{2,1,0:T(8,128)S(1)} %all-to-all-done.y_ref, f32[128,128]{1,0:T(8,128)S(1)} %copy-done.6, ...), custom_call_target="tpu_custom_call" | custom-call | tf_op jit(solution)/shard_map/pallas_call | solution.py:268
  118.9 18.6 %all_to_all.10 = f32[8,5,32,128]{3,2,1,0:T(8,128)S(1)} all-to-all(f32[8,5,32,128]{3,2,1,0:T(8,128)S(1)} %shard_map.78), channel_id=1, replica_groups=mesh['x'=4,'zlo'=2,'zhi'=2,'y'=4,'core'=2] {'zhi','y'}, dimensions={0} | all-to-all | bytes 1310720 | tf_op jit(solution)/shard_map/all_to_all | solution.py:355
  137.5 0.7 reduce_sum.9
  (9 shorter events, 0.0 us)
Async XLA Ops:
  0.0 48.8 %collective-permute-start.1 = (f32[128,4096]{1,0:T(8,128)}, f32[128,4096]{1,0:T(8,128)S(1)}, u32[]{:S(2)}, u32[]{:S(2)}) collective-permute-start(f32[128,4096]{1,0:T(8,128)} %bitcast.15), channel_id=1, source_target_pairs={{0,1},{1,0},{2,3},{3,2},{4,5},{5,4},{6,7},{7,6},{8,9},{9,8},{10,11... | collective-permute-start | bytes 6291464 | tf_op jit(solution)/shard_map/ppermute | solution.py:42
  0.0 1.2 copy-start.1
  1.4 3.3 %collective-permute-start.2 = (bf16[16,64,128]{2,1,0:T(8,128)(2,1)S(1)}, bf16[16,64,128]{2,1,0:T(8,128)(2,1)S(1)}, u32[]{:S(2)}, u32[]{:S(2)}) collective-permute-start(bf16[16,64,128]{2,1,0:T(8,128)(2,1)S(1)} %shard_map.66), channel_id=1, source_target_pairs={{0,1},{1,0},{2,3},{3,2},{4,5},{5,4},{6,7},{7,6},{8,9},{9,8},{10,11... | collective-permute-start | bytes 786440 | tf_op jit(solution)/shard_map/ppermute | solution.py:42
  2.0 1.2 copy-start.2
  4.9 11.5 %collective-permute-start.6 = (bf16[1,16,64,128]{3,2,1,0:T(8,128)(2,1)S(1)}, bf16[1,16,64,128]{3,2,1,0:T(8,128)(2,1)}, u32[]{:S(2)}, u32[]{:S(2)}) collective-permute-start(bf16[1,16,64,128]{3,2,1,0:T(8,128)(2,1)S(1)} %get-tuple-element.10), channel_id=1, source_target_pairs={{0,4},{1,5},{2,6},{3,7},{4,0},{5,1},{6,2},{7,3},{8,12},{9,13},{10,... | collective-permute-start | bytes 786440 | tf_op jit(solution)/shard_map/ppermute | solution.py:42
  8.3 11.7 %collective-permute-start.12 = (bf16[2,8,64,128]{3,2,1,0:T(8,128)(2,1)S(1)}, bf16[2,8,64,128]{3,2,1,0:T(8,128)(2,1)S(1)}, u32[]{:S(2)}, u32[]{:S(2)}) collective-permute-start(bf16[2,8,64,128]{3,2,1,0:T(8,128)(2,1)S(1)} %get-tuple-element.12), channel_id=1, source_target_pairs={{0,24},{1,25},{2,26},{3,27},{4,28},{5,29},{6,30},{7,31},{8,16},{9,... | collective-permute-start | bytes 786440 | tf_op jit(solution)/shard_map/ppermute | solution.py:42
  12.3 16.8 %collective-permute-start.10 = (bf16[2,16,64,128]{3,2,1,0:T(8,128)(2,1)S(1)}, bf16[2,16,64,128]{3,2,1,0:T(8,128)(2,1)S(1)}, u32[]{:S(2)}, u32[]{:S(2)}) collective-permute-start(bf16[2,16,64,128]{3,2,1,0:T(8,128)(2,1)S(1)} %get-tuple-element.11.rest_0_), channel_id=1, source_target_pairs={{0,2},{1,3},{2,4},{3,5},{4,6},{5,7},{6,0},{7,1},{8,10},{9,11},{10,... | collective-permute-start | bytes 1572872 | tf_op jit(solution)/shard_map/ppermute | solution.py:42
  13.0 16.8 %collective-permute-start.11 = (bf16[2,16,64,128]{3,2,1,0:T(8,128)(2,1)S(1)}, bf16[2,16,64,128]{3,2,1,0:T(8,128)(2,1)S(1)}, u32[]{:S(2)}, u32[]{:S(2)}) collective-permute-start(bf16[2,16,64,128]{3,2,1,0:T(8,128)(2,1)S(1)} %get-tuple-element.11.rest_0_), channel_id=1, source_target_pairs={{0,6},{1,7},{2,0},{3,1},{4,2},{5,3},{6,4},{7,5},{8,14},{9,15},{10,... | collective-permute-start | bytes 1572872 | tf_op jit(solution)/shard_map/ppermute | solution.py:42
  15.6 0.8 copy-start.4
  16.4 8.6 %collective-permute-start.3 = (bf16[2,8,64,128]{3,2,1,0:T(8,128)(2,1)S(1)}, bf16[2,8,64,128]{3,2,1,0:T(8,128)(2,1)}, u32[]{:S(2)}, u32[]{:S(2)}) collective-permute-start(bf16[2,8,64,128]{3,2,1,0:T(8,128)(2,1)S(1)} %get-tuple-element.9), channel_id=1, source_target_pairs={{0,24},{1,25},{2,26},{3,27},{4,28},{5,29},{6,30},{7,31},{8,16},{9,... | collective-permute-start | bytes 786440 | tf_op jit(solution)/shard_map/ppermute | solution.py:42
  20.0 8.0 %collective-permute-start.8 = (bf16[1,16,64,128]{3,2,1,0:T(8,128)(2,1)}, bf16[1,16,64,128]{3,2,1,0:T(8,128)(2,1)}, u32[]{:S(2)}, u32[]{:S(2)}) collective-permute-start(bf16[1,16,64,128]{3,2,1,0:T(8,128)(2,1)} %collective-permute-done.6.rest_2_), channel_id=1, source_target_pairs={{0,32},{1,33},{2,34},{3,35},{4,36},{5,37},{6,38},{7,39},{8,40},{9,... | collective-permute-start | bytes 786440 | tf_op jit(solution)/shard_map/ppermute | solution.py:42
  25.0 10.4 %collective-permute-start.7 = (bf16[1,16,64,128]{3,2,1,0:T(8,128)(2,1)}, bf16[1,16,64,128]{3,2,1,0:T(8,128)(2,1)}, u32[]{:S(2)}, u32[]{:S(2)}) collective-permute-start(bf16[1,16,64,128]{3,2,1,0:T(8,128)(2,1)} %collective-permute-done.6.rest_2_), channel_id=1, source_target_pairs={{0,24},{1,25},{2,26},{3,27},{4,28},{5,29},{6,30},{7,31},{8,16},{9,... | collective-permute-start | bytes 786440 | tf_op jit(solution)/shard_map/ppermute | solution.py:42
  28.0 14.5 %collective-permute-start.9 = (bf16[1,16,64,128]{3,2,1,0:T(8,128)(2,1)}, bf16[1,16,64,128]{3,2,1,0:T(8,128)(2,1)}, u32[]{:S(2)}, u32[]{:S(2)}) collective-permute-start(bf16[1,16,64,128]{3,2,1,0:T(8,128)(2,1)} %collective-permute-done.8.rest_3_), channel_id=1, source_target_pairs={{0,24},{1,25},{2,26},{3,27},{4,28},{5,29},{6,30},{7,31},{8,16},{9,... | collective-permute-start | bytes 786440 | tf_op jit(solution)/shard_map/ppermute | solution.py:42
  29.1 16.3 %collective-permute-start.4 = (bf16[2,8,64,128]{3,2,1,0:T(8,128)(2,1)}, bf16[2,8,64,128]{3,2,1,0:T(8,128)(2,1)}, u32[]{:S(2)}, u32[]{:S(2)}) collective-permute-start(bf16[2,8,64,128]{3,2,1,0:T(8,128)(2,1)} %collective-permute-done.3.rest_0_), channel_id=1, source_target_pairs={{0,2},{1,3},{2,4},{3,5},{4,6},{5,7},{6,0},{7,1},{8,10},{9,11},{10,... | collective-permute-start | bytes 786440 | tf_op jit(solution)/shard_map/ppermute | solution.py:42
  29.8 17.5 %collective-permute-start.5 = (bf16[2,8,64,128]{3,2,1,0:T(8,128)(2,1)}, bf16[2,8,64,128]{3,2,1,0:T(8,128)(2,1)}, u32[]{:S(2)}, u32[]{:S(2)}) collective-permute-start(bf16[2,8,64,128]{3,2,1,0:T(8,128)(2,1)} %collective-permute-done.3.rest_0_), channel_id=1, source_target_pairs={{0,6},{1,7},{2,0},{3,1},{4,2},{5,3},{6,4},{7,5},{8,14},{9,15},{10,... | collective-permute-start | bytes 786440 | tf_op jit(solution)/shard_map/ppermute | solution.py:42
  35.4 44.1 %collective-permute-start.16 = (bf16[512,5,8,128]{3,2,1,0:T(8,128)(2,1)}, bf16[512,5,8,128]{3,2,1,0:T(8,128)(2,1)}, u32[]{:S(2)}, u32[]{:S(2)}) collective-permute-start(bf16[512,5,8,128]{3,2,1,0:T(8,128)(2,1)} %bitcast.11), channel_id=1, source_target_pairs={{0,1},{1,0},{2,3},{3,2},{4,5},{5,4},{6,7},{7,6},{8,9},{9,8},{10,11... | collective-permute-start | bytes 15728648 | tf_op jit(solution)/shard_map/ppermute | solution.py:42
  35.4 1.0 copy-start.5
  42.5 14.1 %collective-permute-start.13 = (bf16[2,8,64,128]{3,2,1,0:T(8,128)(2,1)S(1)}, bf16[2,8,64,128]{3,2,1,0:T(8,128)(2,1)S(1)}, u32[]{:S(2)}, u32[]{:S(2)}) collective-permute-start(bf16[2,8,64,128]{3,2,1,0:T(8,128)(2,1)S(1)} %collective-permute-done.12.rest_1_), channel_id=1, source_target_pairs={{0,2},{1,3},{2,4},{3,5},{4,6},{5,7},{6,0},{7,1},{8,10},{9,11},{10,... | collective-permute-start | bytes 786440 | tf_op jit(solution)/shard_map/ppermute | solution.py:42
  45.4 3.4 %copy-start.3 = (f32[4096,8,16]{0,2,1:T(8,128)S(1)}, f32[4096,8,16]{0,2,1:T(8,128)}, u32[]{:S(2)}) copy-start(f32[4096,8,16]{0,2,1:T(8,128)} %param.6) | copy-start | bytes 6291460
  45.4 11.2 %collective-permute-start.14 = (bf16[2,8,64,128]{3,2,1,0:T(8,128)(2,1)S(1)}, bf16[2,8,64,128]{3,2,1,0:T(8,128)(2,1)S(1)}, u32[]{:S(2)}, u32[]{:S(2)}) collective-permute-start(bf16[2,8,64,128]{3,2,1,0:T(8,128)(2,1)S(1)} %collective-permute-done.12.rest_1_), channel_id=1, source_target_pairs={{0,6},{1,7},{2,0},{3,1},{4,2},{5,3},{6,4},{7,5},{8,14},{9,15},{10,... | collective-permute-start | bytes 786440 | tf_op jit(solution)/shard_map/ppermute | solution.py:42
  67.3 4.9 %collective-permute-start.15 = (f32[8,256,256]{2,1,0:T(8,128)S(1)}, f32[8,256,256]{2,1,0:T(8,128)S(1)}, u32[]{:S(2)}, u32[]{:S(2)}) collective-permute-start(f32[8,256,256]{2,1,0:T(8,128)S(1)} %shard_map.77), channel_id=1, source_target_pairs={{0,1},{1,0},{2,3},{3,2},{4,5},{5,4},{6,7},{7,6},{8,9},{9,8},{10,11... | collective-permute-start | bytes 6291464 | tf_op jit(solution)/shard_map/ppermute | solution.py:42
  72.1 5.9 %copy-start.7 = (f32[8]{0:T(128)S(1)}, f32[8]{0:T(128)}, u32[]{:S(2)}) copy-start(f32[8]{0:T(128)} %param.8) | copy-start | bytes 100
  72.1 38.0 %copy-start.6 = (f32[128,128]{1,0:T(8,128)S(1)}, f32[128,128]{1,0:T(8,128)}, u32[]{:S(2)}) copy-start(f32[128,128]{1,0:T(8,128)} %v_ref.1) | copy-start | bytes 196612
  73.7 36.4 %all-to-all-start = ((f32[8,256,256]{2,1,0:T(8,128)}), f32[8,256,256]{2,1,0:T(8,128)S(1)}, u32[]{:S(2)}, u32[]{:S(2)}) async-start(f32[8,256,256]{2,1,0:T(8,128)} %add.168), calls=%async_computation | async-start | bytes 4194304 | tf_op jit(solution)/shard_map/all_to_all | solution.py:353
  78.1 1.5 %collective-permute-start = (f32[8]{0:T(128)S(1)}, f32[8]{0:T(128)S(1)}, u32[]{:S(2)}, u32[]{:S(2)}) collective-permute-start(f32[8]{0:T(128)S(1)} %broadcast_multiply_fusion.w_own_ref), channel_id=1, source_target_pairs={{0,1},{1,0},{2,3},{3,2},{4,5},{5,4},{6,7},{7,6},{8,9},{9,8},{10,11... | collective-permute-start | bytes 104 | tf_op jit(solution)/shard_map/ppermute | solution.py:42
  110.1 2.5 %copy-start = (bf16[512,8,5,128]{3,1,2,0:T(8,128)(2,1)S(1)}, bf16[512,8,5,128]{3,1,2,0:T(8,128)(2,1)}, u32[]{:S(2)}) copy-start(bf16[512,8,5,128]{3,1,2,0:T(8,128)(2,1)} %param.7) | copy-start | bytes 15728644
